TPU v7x, 128 devices: a whole 4x4x4 slice. The times are simulated.
128 devices in a mesh: row: 32 (over z, y, core), col: 4 (over x).
Axes of the slice: x: 4, y: 4, z: 4, core: 2. Of those that a mesh axis runs over, the one named last changes fastest.
Arguments:
- tokens: bfloat16 [16384, 2048], P('row', 'col'), may hold values from -6 to 6
- cotangent: bfloat16 [16384, 2048], P('row', 'col'), may hold values from -6 to 6
- destination: int32 [16384], P('row'), may hold values from 0 to 16383, as said below
- segment_ids: int32 [16384], P('row'), may hold values from 0 to 7, as said below
- attn_gain: float32 [2048], replicated, may hold values from 0.5 to 1.5
- w_query: bfloat16 [2048, 2048], P('row', 'col'), may hold values from -0.125 to 0.125
- w_key: bfloat16 [2048, 256], P('row', 'col'), may hold values from -0.125 to 0.125
- w_value: bfloat16 [2048, 256], P('row', 'col'), may hold values from -0.125 to 0.125
- w_output: bfloat16 [2048, 2048], P('row', 'col'), may hold values from -0.5 to 0.5
- ffn_gain: float32 [2048], replicated, may hold values from 0.5 to 1.5
- w_gate: bfloat16 [2048, 5632], P('row', 'col'), may hold values from -0.125 to 0.125
- w_up: bfloat16 [2048, 5632], P('row', 'col'), may hold values from -0.125 to 0.125
- w_down: bfloat16 [2048, 5632], P('row', 'col'), may hold values from -0.078125 to 0.078125
Outputs:
- output: bfloat16 [16384, 2048], P('row', 'col')
- input_grad: bfloat16 [16384, 2048], P('row', 'col')
- attn_gain_grad: float32 [2048], P('row')
- w_query_grad: float32 [2048, 2048], P('row', 'col')
- w_key_grad: float32 [2048, 256], P('row', 'col')
- w_value_grad: float32 [2048, 256], P('row', 'col')
- w_output_grad: float32 [2048, 2048], P('row', 'col')
- ffn_gain_grad: float32 [2048], P('row')
- w_gate_grad: float32 [2048, 5632], P('row', 'col')
- w_up_grad: float32 [2048, 5632], P('row', 'col')
- w_down_grad: float32 [2048, 5632], P('row', 'col')
Inputs may be any that keep to these rules, and one draw needn't show every extreme that they name: `destination`: A permutation; the tokens of each aligned block of 512 arriving tokens go to exactly 16 places in each aligned block of 512 balanced places. `segment_ids`: within each aligned block of 512 places the ids start at 0 and rise by one where a new sequence begins, so a block holds at most 8 sequences; in every draw some block holds a single sequence of 512 tokens and some block holds 8 sequences.
All inputs are finite; a program needn't handle non-finite values.
Results may differ from a plain program's by a relative error of at most 0.028.
Values may be sent and summed in bfloat16 or wider, within the bound.
No kernel may reach another device: no remote copies, remote signals or barrier semaphores. Data moves between devices by JAX's collectives and lax.ppermute only.
A program may use at most 128 MiB of HBM per device.

v0:
```python
from functools import partial
import jax
import jax.numpy as jnp
from jax import lax
from jax.sharding import PartitionSpec as P

HEADS = 32
KV = 4
HD = 64
EPS = 1e-05
ROPE_BASE = 10000.0


def rope_tables(positions):
    half_width = HD // 2
    freqs = ROPE_BASE ** (-(jnp.arange(half_width, dtype=jnp.float32) * 2.0 / HD))
    angles = positions.astype(jnp.float32)[:, None] * freqs[None, :]
    return (jnp.cos(angles)[:, None, :], jnp.sin(angles)[:, None, :])


def rotate(values, cosine, sine):
    half_width = values.shape[-1] // 2
    first = values[..., :half_width]
    second = values[..., half_width:]
    return jnp.concatenate(
        [first * cosine - second * sine, second * cosine + first * sine], axis=-1
    )


def rotate_back(grads, cosine, sine):
    half_width = grads.shape[-1] // 2
    first = grads[..., :half_width]
    second = grads[..., half_width:]
    return jnp.concatenate(
        [first * cosine + second * sine, second * cosine - first * sine], axis=-1
    )


def positions_of(segment_ids):
    index = jnp.arange(segment_ids.shape[0], dtype=jnp.int32)
    change = jnp.concatenate([jnp.ones((1,), dtype=jnp.bool_), segment_ids[1:] != segment_ids[:-1]])
    starts = jnp.where(change, index, jnp.zeros_like(index))
    return index - lax.cummax(starts, axis=0)


def allowed_pairs(segment_ids):
    index = jnp.arange(segment_ids.shape[0], dtype=jnp.int32)
    return (segment_ids[:, None] == segment_ids[None, :]) & (index[None, :] <= index[:, None])


def rms_scale(values):
    return lax.rsqrt(jnp.mean(values * values, axis=-1, keepdims=True) + EPS)


def norm_back(values, inv_root, gain, grads):
    normed = values * inv_root
    scaled = grads * gain
    result = inv_root * (scaled - normed * jnp.mean(scaled * normed, axis=-1, keepdims=True))
    return (result, jnp.sum(grads * normed, axis=0))


def matmul(left, right):
    return jnp.dot(left, right, preferred_element_type=jnp.float32)


def head_scores(query_head, key_head, allowed, scale_factor):
    scores = matmul(query_head, key_head.T) * scale_factor
    return jnp.where(allowed, scores, -1e30)


def head_forward(inputs, key_heads, value_heads, allowed, scale_factor):
    query_head, kv_slot = inputs
    scores = head_scores(query_head, key_heads[kv_slot], allowed, scale_factor)
    peak = jnp.max(scores, axis=-1, keepdims=True)
    expo = jnp.exp(scores - peak)
    total = jnp.sum(expo, axis=-1, keepdims=True)
    probs = expo / total
    mixed = matmul(probs.astype(jnp.bfloat16), value_heads[kv_slot])
    return (mixed, (peak + jnp.log(total))[:, 0])


def head_backward(inputs, key_heads, value_heads, allowed, scale_factor):
    query_head, kv_slot, grad_head, log_total = inputs
    key_head = key_heads[kv_slot]
    value_head = value_heads[kv_slot]
    scores = head_scores(query_head, key_head, allowed, scale_factor)
    probs = jnp.exp(scores - log_total[:, None])
    prob_grad = matmul(grad_head, value_head.T)
    value_grad = matmul(probs.astype(jnp.bfloat16).T, grad_head)
    inner = jnp.sum(probs * prob_grad, axis=-1, keepdims=True)
    score_grad = (probs * (prob_grad - inner)).astype(jnp.bfloat16)
    query_grad = matmul(score_grad, key_head) * scale_factor
    key_grad = matmul(score_grad.T, query_head) * scale_factor
    return (query_grad, key_grad, value_grad)


def gather_rows(parts):
    widths = [part.shape[1] for part in parts]
    packed = lax.all_gather(jnp.concatenate(parts, axis=1), "row", axis=0, tiled=True)
    pieces = []
    offset = 0
    for width in widths:
        pieces.append(packed[:, offset : offset + width])
        offset += width
    return pieces


def scatter_rows(parts):
    columns = [part.reshape(part.shape[0], -1).astype(jnp.bfloat16) for part in parts]
    widths = [column.shape[1] for column in columns]
    packed = lax.psum_scatter(
        jnp.concatenate(columns, axis=1), "row", scatter_dimension=0, tiled=True
    ).astype(jnp.float32)
    pieces = []
    offset = 0
    for part, width in zip(parts, widths):
        piece = packed[:, offset : offset + width]
        pieces.append(piece.reshape(-1) if part.ndim == 1 else piece)
        offset += width
    return pieces


def body(
    tokens,
    cotangent,
    destination,
    segment_ids,
    attn_gain,
    w_query,
    w_key,
    w_value,
    w_output,
    ffn_gain,
    w_gate,
    w_up,
    w_down,
):
    row_count = tokens.shape[0]
    quarter = tokens.shape[1]
    col_start = lax.axis_index("col") * quarter
    group_size = HEADS // KV
    send_order = jnp.argsort(destination)
    slot_ids = destination[send_order] % row_count
    arrived_rows, arrived_grads, arrived_slots = (
        lax.all_to_all(tokens[send_order], "row", split_axis=0, concat_axis=0, tiled=True),
        lax.all_to_all(cotangent[send_order], "row", split_axis=0, concat_axis=0, tiled=True),
        lax.all_to_all(slot_ids, "row", split_axis=0, concat_axis=0, tiled=True),
    )
    placing = jnp.argsort(arrived_slots)
    full_rows, full_grads = (
        lax.all_gather(arrived_rows[placing], "col", axis=1, tiled=True),
        lax.all_gather(arrived_grads[placing], "col", axis=1, tiled=True),
    )
    query_w, key_w, value_w, output_w = gather_rows([w_query, w_key, w_value, w_output])
    cosine, sine = rope_tables(positions_of(segment_ids))
    allowed = allowed_pairs(segment_ids)
    rows_wide = full_rows.astype(jnp.float32)
    inv_one = rms_scale(rows_wide)
    normed_one = (rows_wide * inv_one * attn_gain).astype(jnp.bfloat16)
    query = matmul(normed_one, query_w)
    key_raw = matmul(normed_one, key_w)
    value_raw = matmul(normed_one, value_w)
    query_heads_count = query.shape[1] // HD
    kv_count = key_raw.shape[1] // HD
    query_rot = (
        rotate(query.reshape(row_count, query_heads_count, HD), cosine, sine)
        .astype(jnp.bfloat16)
        .transpose(1, 0, 2)
    )
    key_rot = (
        rotate(key_raw.reshape(row_count, kv_count, HD), cosine, sine)
        .astype(jnp.bfloat16)
        .transpose(1, 0, 2)
    )
    value_heads = value_raw.astype(jnp.bfloat16).reshape(row_count, kv_count, HD).transpose(1, 0, 2)
    kv_slots = jnp.arange(query_heads_count, dtype=jnp.int32) // group_size
    scale_factor = HD ** (-0.5)
    mixed_heads, log_totals = lax.map(
        partial(
            head_forward,
            key_heads=key_rot,
            value_heads=value_heads,
            allowed=allowed,
            scale_factor=scale_factor,
        ),
        (query_rot, kv_slots),
    )
    mixed = (
        mixed_heads.transpose(1, 0, 2)
        .reshape(row_count, query_heads_count * HD)
        .astype(jnp.bfloat16)
    )
    attn_terms = matmul(mixed, output_w.T)
    attn_full = lax.psum(attn_terms, "col")
    resid = rows_wide + attn_full
    inv_two = rms_scale(resid)
    normed_two = (resid * inv_two * ffn_gain).astype(jnp.bfloat16)
    resid_part = lax.dynamic_slice_in_dim(resid, col_start, quarter, 1)
    gate_w, up_w, down_w = gather_rows([w_gate, w_up, w_down])
    gate = matmul(normed_two, gate_w)
    upper = matmul(normed_two, up_w)
    sigmoid_gate = jax.nn.sigmoid(gate)
    activ = (gate * sigmoid_gate * upper).astype(jnp.bfloat16)
    ffn_share = lax.psum_scatter(
        matmul(activ, down_w.T).astype(jnp.bfloat16), "col", scatter_dimension=1, tiled=True
    ).astype(jnp.float32)
    output_share = (resid_part + ffn_share).astype(jnp.bfloat16)
    down_weight_grad = matmul(full_grads.T, activ)
    act_grad = matmul(full_grads, down_w)
    gate_grad = (act_grad * upper * sigmoid_gate * (1.0 + gate * (1.0 - sigmoid_gate))).astype(
        jnp.bfloat16
    )
    up_grad = (act_grad * gate * sigmoid_gate).astype(jnp.bfloat16)
    gate_weight_grad = matmul(normed_two.T, gate_grad)
    up_weight_grad = matmul(normed_two.T, up_grad)
    normed_terms_two = matmul(gate_grad, gate_w.T) + matmul(up_grad, up_w.T)
    normed_grad_two = lax.psum(normed_terms_two, "col")
    resid_norm_grad, ffn_gain_grad = norm_back(resid, inv_two, ffn_gain, normed_grad_two)
    resid_grad = full_grads.astype(jnp.float32) + resid_norm_grad
    attn_grad_low = resid_grad.astype(jnp.bfloat16)
    output_weight_grad = matmul(attn_grad_low.T, mixed)
    mixed_grad = matmul(attn_grad_low, output_w).astype(jnp.bfloat16)
    mixed_grad_heads = mixed_grad.reshape(row_count, query_heads_count, HD).transpose(1, 0, 2)
    query_grads, key_grads, value_grads = lax.map(
        partial(
            head_backward,
            key_heads=key_rot,
            value_heads=value_heads,
            allowed=allowed,
            scale_factor=scale_factor,
        ),
        (query_rot, kv_slots, mixed_grad_heads, log_totals),
    )
    query_grad = (
        rotate_back(query_grads.transpose(1, 0, 2), cosine, sine)
        .reshape(row_count, query_heads_count * HD)
        .astype(jnp.bfloat16)
    )
    key_sum = key_grads.reshape(kv_count, group_size, row_count, HD).sum(axis=1).transpose(1, 0, 2)
    key_grad = (
        rotate_back(key_sum, cosine, sine).reshape(row_count, kv_count * HD).astype(jnp.bfloat16)
    )
    value_sum = (
        value_grads.reshape(kv_count, group_size, row_count, HD).sum(axis=1).transpose(1, 0, 2)
    )
    value_grad = value_sum.reshape(row_count, kv_count * HD).astype(jnp.bfloat16)
    query_weight_grad = matmul(normed_one.T, query_grad)
    key_weight_grad = matmul(normed_one.T, key_grad)
    value_weight_grad = matmul(normed_one.T, value_grad)
    normed_terms_one = (
        matmul(query_grad, query_w.T) + matmul(key_grad, key_w.T) + matmul(value_grad, value_w.T)
    )
    normed_grad_one = lax.psum(normed_terms_one.astype(jnp.bfloat16), "col").astype(jnp.float32)
    rows_norm_grad, attn_gain_grad = norm_back(rows_wide, inv_one, attn_gain, normed_grad_one)
    rows_grad = resid_grad + rows_norm_grad
    input_share = lax.dynamic_slice_in_dim(rows_grad, col_start, quarter, 1).astype(jnp.bfloat16)
    (
        query_result,
        key_result,
        value_result,
        output_result,
        gate_result,
        up_result,
        down_result,
        attn_gain_result,
        ffn_gain_result,
    ) = scatter_rows(
        [
            query_weight_grad,
            key_weight_grad,
            value_weight_grad,
            output_weight_grad,
            gate_weight_grad,
            up_weight_grad,
            down_weight_grad,
            attn_gain_grad,
            ffn_gain_grad,
        ]
    )
    back_rows, back_grads = (
        lax.all_to_all(output_share[arrived_slots], "row", split_axis=0, concat_axis=0, tiled=True),
        lax.all_to_all(input_share[arrived_slots], "row", split_axis=0, concat_axis=0, tiled=True),
    )
    restore = jnp.argsort(send_order)
    return (
        back_rows[restore],
        back_grads[restore],
        attn_gain_result,
        query_result,
        key_result,
        value_result,
        output_result,
        ffn_gain_result,
        gate_result,
        up_result,
        down_result,
    )


def solution(mesh):
    placed = (
        P("row", "col"),
        P("row", "col"),
        P("row"),
        P("row"),
        P(),
        P("row", "col"),
        P("row", "col"),
        P("row", "col"),
        P("row", "col"),
        P(),
        P("row", "col"),
        P("row", "col"),
        P("row", "col"),
    )
    return jax.shard_map(
        body,
        mesh=mesh,
        in_specs=placed,
        out_specs=(
            P("row", "col"),
            P("row", "col"),
            P("row"),
            P("row", "col"),
            P("row", "col"),
            P("row", "col"),
            P("row", "col"),
            P("row"),
            P("row", "col"),
            P("row", "col"),
            P("row", "col"),
        ),
        check_vma=False,
    )
```

profile of v0, /device:TPU:1, one launch (start us, length us, event | category | flops | bytes accessed | tf_op | source)
XLA Modules:
  0.0 914.6 jit_solution(13303859457156370730)
XLA Ops:
  7.2 4.5 sort.45
  12.3 3.6 gather_fusion.1
  16.6 9.6 %all-to-all-start.1 = ((s32[32,16,1]{1,2,0:T(1,128)}), s32[32,16,1]{1,2,0:T(1,128)S(1)}, u32[]{:S(2)}, u32[]{:S(2)}) async-start(s32[32,16,1]{1,2,0:T(1,128)} %bitcast.2), calls=%async_computation.1 | async-start | bytes 32768 | tf_op jit(solution)/shard_map/all_to_all | solution.py:147
  26.2 2.6 gather_fusion
  28.9 4.2 all-to-all-done.1
  33.1 4.2 all-to-all-start
  38.6 3.8 sort.46
  42.4 6.5 all-to-all-done
  48.9 2.6 gather_fusion.2
  53.7 26.4 %all-gather.11.cloned.1.call-done = bf16[512,2048]{1,0:T(8,128)(2,1)} async-done(((bf16[512,512]{1,0:T(8,128)(2,1)}), bf16[512,2048]{1,0:T(8,128)(2,1)}) %all-gather.11.cloned.1.call-update) | async-done | bytes 2097168 | tf_op jit(solution)/shard_map/all_gather | solution.py:151
  80.0 2.1 fusion.54
  82.1 48.2 %all-gather.7.cloned.1.call-done = bf16[2048,1152]{1,0:T(8,128)(2,1)} async-done(((bf16[64,1152]{1,0:T(8,128)(2,1)}), bf16[2048,1152]{1,0:T(8,128)(2,1)}) %all-gather.7.cloned.1.call-update) | async-done | bytes 4718608 | tf_op jit(solution)/shard_map/all_gather | solution.py:99
  130.3 3.6 fusion.67
  135.6 1.9 convolution_bitcast_fusion.2
  138.0 2.0 fusion.72
  140.1 25.1 %while.32 = (s32[]{:T(128)}, bf16[8,512,64]{1,2,0:T(8,128)(2,1)S(1)}, f32[8,512]{1,0:T(8,128)}, bf16[8,512,64]{2,1,0:T(8,128)(2,1)}, bf16[1,512,64]{2,1,0:T(8,12...) while((s32[]{:T(128)}, bf16[8,512,64]{1,2,0:T(8,128)(2,1)S(1)}, ...), condition=%wide.region_8.9_spmd.clone.clone, body=%wide.region_5.8_spmd.clone.sunk.clone | while | flops 69991936 | bytes 3694689 | solution.py:178
  166.0 5.0 fusion.63
  172.0 2.0 gather_fusion.5
  174.0 16.6 %all_to_all.60 = bf16[32,16,512]{2,1,0:T(8,128)(2,1)S(1)} all-to-all(bf16[32,16,512]{2,1,0:T(8,128)(2,1)S(1)} %bitcast.184), channel_id=1, replica_groups=mesh['row'=32,'col'=4] {'row'}, dimensions={0} | all-to-all | bytes 1048576 | tf_op jit(solution)/shard_map/all_to_all | solution.py:146
  190.6 2.6 gather_fusion.6
  195.2 67.6 %all-reduce.4.cloned.1.call-done = f32[512,2048]{1,0:T(8,128)} async-done(((f32[512,2048]{1,0:T(8,128)}), f32[512,2048]{1,0:T(8,128)}) %all-reduce.4.cloned.1.call-update) | async-done | bytes 4194320 | tf_op jit(solution)/shard_map/psum | solution.py:194
  262.7 2.8 multiply_reduce_fusion.4
  265.6 2.0 copy-done.2
  269.3 26.3 %all-gather.13.cloned.1.call-done = bf16[512,2048]{1,0:T(8,128)(2,1)} async-done(((bf16[512,512]{1,0:T(8,128)(2,1)}), bf16[512,2048]{1,0:T(8,128)(2,1)}) %all-gather.13.cloned.1.call-update) | async-done | bytes 2097168 | tf_op jit(solution)/shard_map/all_gather | solution.py:152
  295.7 76.7 %all-gather.9.cloned.1.call-done = bf16[2048,4224]{1,0:T(8,128)(2,1)} async-done(((bf16[64,4224]{1,0:T(8,128)(2,1)}), bf16[2048,4224]{1,0:T(8,128)(2,1)}) %all-gather.9.cloned.1.call-update) | async-done | bytes 17301520 | tf_op jit(solution)/shard_map/all_gather | solution.py:99
  372.4 6.5 fusion.41
  378.9 2.3 copy-done.31
  381.3 5.0 fusion.47
  386.2 7.3 multiply_convert_fusion.4
  393.6 5.4 fusion.45
  398.9 5.0 fusion.55
  404.0 9.7 %all-reduce.8.cloned.1.call-start = ((), (), s32[]{:S(2)}) async-start(), calls=%async_computation.12 | async-start | bytes 4194304 | tf_op jit(solution)/shard_map/psum | solution.py:253
  413.7 82.1 %all-reduce.6.cloned.1.call-done = f32[512,2048]{1,0:T(8,128)} async-done(((f32[512,2048]{1,0:T(8,128)}), f32[512,2048]{1,0:T(8,128)}) %all-reduce.6.cloned.1.call-update) | async-done | bytes 4194320 | tf_op jit(solution)/shard_map/psum | solution.py:217
  495.9 4.6 multiply_reduce_fusion.1
  501.8 2.7 multiply_add_fusion
  504.5 1.9 copy-done.7
  506.4 3.7 fusion.69
  511.6 50.9 %while.33 = (s32[]{:T(128)}, f32[8,512,64]{1,2,0:T(8,128)}, f32[8,512,64]{1,2,0:T(8,128)}, f32[8,512,64]{1,2,0:T(8,128)}, bf16[8,512,64]{2,1,0:T(8,128)(2,1)}, /...) while((s32[]{:T(128)}, f32[8,512,64]{1,2,0:T(8,128)}, ...), condition=%wide.region_17.18_spmd.clone.clone, body=%wide.region_15.17_spmd.clone.sunk.clone | while | flops 170982912 | bytes 9126013 | solution.py:224
  540.6 1.9 fusion.176
  567.5 2.9 fusion.65
  572.2 3.2 add_convert_fusion
  575.5 7.9 fusion.58
  583.5 7.9 convolution_convert_fusion.2
  591.4 5.3 convolution_convert_fusion.1
  596.7 5.0 convolution_convert_fusion
  603.4 2.7 convolution_convert_fusion.4
  606.1 2.6 convolution_convert_fusion.3
  608.7 25.4 %all-reduce.8.cloned.1.call-done = bf16[512,2048]{1,0:T(8,128)(2,1)} async-done(((bf16[512,2048]{1,0:T(8,128)(2,1)}), bf16[512,2048]{1,0:T(8,128)(2,1)}) %all-reduce.8.cloned.1.call-update) | async-done | bytes 2097168 | tf_op jit(solution)/shard_map/psum | solution.py:253
  634.1 6.1 fusion.53
  640.2 93.2 %concatenate.53 = bf16[2048,5378]{0,1:T(8,128)(2,1)} concatenate(bf16[2048,512]{0,1:T(8,128)(2,1)} %convolution_convert_fusion.4, bf16[2048,64]{0,1:T(8,128)(2,1)S(1)} %convolution_convert_fusion.6, bf16[2048,64]{0,1:T(8,128)(2,1)S(1)} %convolution_convert_fusion.5, bf16[2048,512]{0,1:T(8,128)(2,1)} %convolution_convert_fusion.3, bf16[2048,1408]{0,1:T(8,128)(2,1)} %convolution_convert_fusion.2, ...), dimensions={1} | concatenate | bytes 44056576 | tf_op jit(solution)/shard_map/concatenate | solution.py:112
  733.5 28.4 %copy.67 = bf16[2048,5378]{1,0:T(8,128)(2,1)} copy(bf16[2048,5378]{0,1:T(8,128)(2,1)} %concatenate.53) | data formatting | bytes 44056576
  764.3 2.6 gather_fusion.3
  766.9 7.7 all-to-all-start.2
  774.6 2.5 fusion.73
  777.1 2.6 gather_fusion.7
  779.8 6.4 all-to-all-done.2
  786.1 4.4 all-to-all-start.4
  790.5 3.8 sort.47
  794.3 2.6 gather_fusion.4
  796.9 5.1 all-to-all-done.4
  802.1 2.6 gather_fusion.8
  804.7 89.5 %reduce-scatter.7.cloned.1.call-done = bf16[64,5378]{1,0:T(8,128)(2,1)} async-done(((bf16[2048,5378]{1,0:T(8,128)(2,1)}), bf16[64,5378]{1,0:T(8,128)(2,1)}) %reduce-scatter.7.cloned.1.call-update) | async-done | bytes 688400
  894.2 2.0 copy.68
  903.6 2.1 copy.64
  (248 shorter events, 109.3 us)
Async XLA Ops:
  7.2 19.0 %copy-start = (bf16[512,512]{1,0:T(8,128)(2,1)S(1)}, bf16[512,512]{1,0:T(8,128)(2,1)}, u32[]{:S(2)}) copy-start(bf16[512,512]{1,0:T(8,128)(2,1)} %param.17) | copy-start | bytes 1572868
  11.7 0.6 copy-start.28
  16.6 16.5 %all-to-all-start.1 = ((s32[32,16,1]{1,2,0:T(1,128)}), s32[32,16,1]{1,2,0:T(1,128)S(1)}, u32[]{:S(2)}, u32[]{:S(2)}) async-start(s32[32,16,1]{1,2,0:T(1,128)} %bitcast.2), calls=%async_computation.1 | async-start | bytes 32768 | tf_op jit(solution)/shard_map/all_to_all | solution.py:147
  28.9 22.8 %copy-start.19 = (bf16[64,512]{1,0:T(8,128)(2,1)S(1)}, bf16[64,512]{1,0:T(8,128)(2,1)}, u32[]{:S(2)}) copy-start(bf16[64,512]{1,0:T(8,128)(2,1)} %param.22) | copy-start | bytes 196612
  28.9 22.8 %copy-start.20 = (bf16[64,512]{1,0:T(8,128)(2,1)S(1)}, bf16[64,512]{1,0:T(8,128)(2,1)}, u32[]{:S(2)}) copy-start(bf16[64,512]{1,0:T(8,128)(2,1)} %param.25) | copy-start | bytes 196612
  28.9 22.8 %copy-start.21 = (bf16[64,64]{1,0:T(8,128)(2,1)S(1)}, bf16[64,64]{1,0:T(8,128)(2,1)}, u32[]{:S(2)}) copy-start(bf16[64,64]{1,0:T(8,128)(2,1)} %param.23) | copy-start | bytes 24580
  28.9 22.8 %copy-start.22 = (bf16[64,64]{1,0:T(8,128)(2,1)S(1)}, bf16[64,64]{1,0:T(8,128)(2,1)}, u32[]{:S(2)}) copy-start(bf16[64,64]{1,0:T(8,128)(2,1)} %param.24) | copy-start | bytes 24580
  28.9 23.7 %copy-start.25 = (s32[512]{0:T(512)S(1)}, s32[512]{0:T(512)}, u32[]{:S(2)}) copy-start(s32[512]{0:T(512)} %param.20) | copy-start | bytes 6148
  33.1 49.0 %copy-start.16 = (s32[32,16,1]{1,2,0:T(1,128)}, s32[32,16,1]{1,2,0:T(1,128)S(1)}, u32[]{:S(2)}) copy-start(s32[32,16,1]{1,2,0:T(1,128)S(1)} %all-to-all-done.1) | copy-start | bytes 6148
  33.1 15.9 %all-to-all-start = ((bf16[32,16,512]{2,1,0:T(8,128)(2,1)}), bf16[32,16,512]{2,1,0:T(8,128)(2,1)S(1)}, u32[]{:S(2)}, u32[]{:S(2)}) async-start(bf16[32,16,512]{2,1,0:T(8,128)(2,1)} %bitcast), calls=%async_computation | async-start | bytes 1048576 | tf_op jit(solution)/shard_map/all_to_all | solution.py:145
  37.3 42.7 %all-gather.11.cloned.1.call-start = ((), (), s32[]{:S(2)}) async-start(), calls=%async_computation.13 | async-start | bytes 2621440 | tf_op jit(solution)/shard_map/all_gather | solution.py:151
  48.9 81.4 %copy-start.23 = (f32[2048]{0:T(1024)S(1)}, f32[2048]{0:T(1024)}, u32[]{:S(2)}) copy-start(f32[2048]{0:T(1024)} %param.21) | copy-start | bytes 24580
  51.6 78.8 %all-gather.7.cloned.1.call-start = ((), (), s32[]{:S(2)}) async-start(), calls=%async_computation.7 | async-start | bytes 4866048 | tf_op jit(solution)/shard_map/all_gather | solution.py:99
  52.5 210.3 %all-reduce.4.cloned.1.call-start = ((), (), s32[]{:S(2)}) async-start(), calls=%async_computation.8 | async-start | bytes 8388608 | tf_op jit(solution)/shard_map/psum | solution.py:194
  53.1 84.4 %copy-start.30 = (f32[32]{0:T(128)}, f32[32]{0:T(128)S(1)}, u32[]{:S(2)}) copy-start(f32[32]{0:T(128)S(1)} %negate_power_fusion) | copy-start | bytes 388
  134.0 1.7 copy-start.5
  135.6 4.5 copy-start.26
  165.2 0.8 copy-start.9
  171.0 1.0 copy-start.4
  171.0 124.6 %all-gather.13.cloned.1.call-start = ((), (), s32[]{:S(2)}) async-start(), calls=%async_computation.14 | async-start | bytes 2621440 | tf_op jit(solution)/shard_map/all_gather | solution.py:152
  190.6 2.7 copy-start.14
  190.6 2.7 copy-start.15
  193.3 179.1 %all-gather.9.cloned.1.call-start = ((), (), s32[]{:S(2)}) async-start(), calls=%async_computation.9 | async-start | bytes 17842176 | tf_op jit(solution)/shard_map/all_gather | solution.py:99
  195.1 72.5 %copy-start.18 = (f32[2048]{0:T(1024)S(1)}, f32[2048]{0:T(1024)}, u32[]{:S(2)}) copy-start(f32[2048]{0:T(1024)} %param.26) | copy-start | bytes 24580
  195.1 300.7 %all-reduce.6.cloned.1.call-start = ((), (), s32[]{:S(2)}) async-start(), calls=%async_computation.11 | async-start | bytes 8388608 | tf_op jit(solution)/shard_map/psum | solution.py:217
  265.6 2.1 copy-start.2
  372.4 6.6 copy-start.11
  372.4 8.9 copy-start.31
  393.6 5.4 copy-start.32
  404.0 230.1 %all-reduce.8.cloned.1.call-start = ((), (), s32[]{:S(2)}) async-start(), calls=%async_computation.12 | async-start | bytes 4194304 | tf_op jit(solution)/shard_map/psum | solution.py:253
  495.9 4.6 copy-start.3
  495.9 5.9 copy-start.6
  504.4 1.9 copy-start.7
  506.4 5.2 copy-start.27
  575.4 187.3 %reduce-scatter.5.cloned.1.call-start = ((), (), s32[]{:S(2)}) async-start(), calls=%async_computation.10 | async-start | bytes 2621440 | tf_op jit(solution)/shard_map/reduce_scatter | solution.py:204
  583.4 310.8 %reduce-scatter.7.cloned.1.call-start = ((), (), s32[]{:S(2)}) async-start(), calls=%async_computation.15 | async-start | bytes 23248896
  583.4 8.0 copy-start.12
  583.5 7.9 copy-start.34
  591.4 5.3 copy-start.13
  591.4 5.3 copy-start.33
  596.7 5.0 copy-start.24
  603.3 2.8 copy-start.8
  603.3 2.7 copy-start.10
  761.9 0.7 copy-start.17
  766.9 19.3 %all-to-all-start.2 = ((bf16[32,16,512]{2,1,0:T(8,128)(2,1)}), bf16[32,16,512]{2,1,0:T(8,128)(2,1)S(1)}, u32[]{:S(2)}, u32[]{:S(2)}) async-start(bf16[32,16,512]{2,1,0:T(8,128)(2,1)} %bitcast.14), calls=%async_computation.3 | async-start | bytes 1048576 | tf_op jit(solution)/shard_map/all_to_all | solution.py:281
  774.6 15.9 %copy-start.29 = (s32[512]{0:T(512)S(1)}, s32[512]{0:T(512)}, u32[]{:S(2)}) copy-start(s32[512]{0:T(512)} %copy-done.28) | copy-start | bytes 6148
  786.1 15.9 %all-to-all-start.4 = ((bf16[32,16,512]{2,1,0:T(8,128)(2,1)}), bf16[32,16,512]{2,1,0:T(8,128)(2,1)S(1)}, u32[]{:S(2)}, u32[]{:S(2)}) async-start(bf16[32,16,512]{2,1,0:T(8,128)(2,1)} %bitcast.24), calls=%async_computation.5 | async-start | bytes 1048576 | tf_op jit(solution)/shard_map/all_to_all | solution.py:282
  897.2 10.4 %copy-start.1 = (bf16[512,512]{1,0:T(8,128)(2,1)S(1)}, bf16[512,512]{1,0:T(8,128)(2,1)}, u32[]{:S(2)}) copy-start(bf16[512,512]{1,0:T(8,128)(2,1)} %param.17) | copy-start | bytes 1572868
Sparse Core Ops, SparseCore 0:
  51.7 28.2 all-gather.10
  82.8 47.4 all-gather.6
  171.1 91.5 all-reduce.3
  264.9 30.6 all-gather.12
  298.0 74.3 all-gather.8
  404.1 91.7 all-reduce.5
  575.6 58.4 all-reduce.7
  636.6 29.4 reduce-scatter.4
  762.0 132.1 reduce-scatter.6
where the time goes:
time: 928 us; the launch traced here: 915 us
  waiting for transfers between devices  465 us (50%)
  local copies, waits for them, and re-layouts  191 us (21%)
  matrix products  142 us (15%)
  other arithmetic  49.6 us (5%)
  starting transfers between devices  36.1 us (4%)
  blocking collectives  16.6 us (2%)
  between operations  14.9 us (2%)
    dot_general x77, matrix products, matmul(): return jnp.dot(left, right, preferred_element_type=jnp.float32)  142 us
    all_gather x2, waiting for transfers between devices, gather_rows(): lax.all_gather(jnp.concatenate(parts, axis=1), 'row', axis=0, tiled=True)  125 us
    concatenate x1, local copies, waits for them, and re-layouts, scatter_rows(): jnp.concatenate(columns, axis=1)  93.2 us
    unnamed x10, waiting for transfers between devices  89.6 us
    psum x1, waiting for transfers between devices, body(): normed_grad_two = lax.psum(normed_terms_two, 'col')  82.1 us
    psum x1, waiting for transfers between devices, body(): attn_full = lax.psum(attn_terms, 'col')  67.6 us
    unnamed x82, local copies, waits for them, and re-layouts  51.5 us
    all_gather x1, waiting for transfers between devices, body(): lax.all_gather(arrived_rows[placing], 'col', axis=1, tiled=True)  26.4 us
  transfers between devices with their start and end apart: 13, of which 12 were waited for; matrix products, arithmetic and copies ran while one was open for 22% of the time, Pallas kernels for 0%

commit v1 on v0

--- a/solution.py
+++ b/solution.py
@@ -250,7 +250,9 @@
     normed_terms_one = (
         matmul(query_grad, query_w.T) + matmul(key_grad, key_w.T) + matmul(value_grad, value_w.T)
     )
-    normed_grad_one = lax.psum(normed_terms_one.astype(jnp.bfloat16), "col").astype(jnp.float32)
+    normed_grad_one = jnp.sum(
+        lax.all_gather(normed_terms_one.astype(jnp.bfloat16), "col"), axis=0
+    ).astype(jnp.float32)
     rows_norm_grad, attn_gain_grad = norm_back(rows_wide, inv_one, attn_gain, normed_grad_one)
     rows_grad = resid_grad + rows_norm_grad
     input_share = lax.dynamic_slice_in_dim(rows_grad, col_start, quarter, 1).astype(jnp.bfloat16)

time: 928 us -> 961 us (1.036)
  waiting for transfers between devices: 465 us -> 490 us
    all_gather x0 -> x1, waiting for transfers between devices: none -> 49.5 us  [body(): lax.all_gather(normed_terms_one.astype(jnp.bfloat16), 'col')]
    psum x1 -> x0, waiting for transfers between devices: 25.4 us -> none  [body(): lax.psum(normed_terms_one.astype(jnp.bfloat16), 'col').astype(jnp.float32)]
    all_gather x0 -> x1, starting transfers between devices: none -> 9.71 us  [body(): lax.all_gather(normed_terms_one.astype(jnp.bfloat16), 'col')]
    psum x1 -> x0, starting transfers between devices: 9.71 us -> none  [body(): lax.psum(normed_terms_one.astype(jnp.bfloat16), 'col').astype(jnp.float32)]
where the time goes in v1:
time: 961 us; the launch traced here: 948 us
  waiting for transfers between devices  490 us (51%)
  local copies, waits for them, and re-layouts  191 us (20%)
  matrix products  142 us (15%)
  other arithmetic  56.9 us (6%)
  starting transfers between devices  35.8 us (4%)
  blocking collectives  16.6 us (2%)
  between operations  14.9 us (2%)
    dot_general x77, matrix products, matmul(): return jnp.dot(left, right, preferred_element_type=jnp.float32)  142 us
    all_gather x2, waiting for transfers between devices, gather_rows(): lax.all_gather(jnp.concatenate(parts, axis=1), 'row', axis=0, tiled=True)  125 us
    concatenate x1, local copies, waits for them, and re-layouts, scatter_rows(): jnp.concatenate(columns, axis=1)  93.2 us
    unnamed x10, waiting for transfers between devices  90.8 us
    psum x1, waiting for transfers between devices, body(): normed_grad_two = lax.psum(normed_terms_two, 'col')  82.1 us
    psum x1, waiting for transfers between devices, body(): attn_full = lax.psum(attn_terms, 'col')  67.5 us
    unnamed x82, local copies, waits for them, and re-layouts  51.5 us
    all_gather x1, waiting for transfers between devices, body(): lax.all_gather(normed_terms_one.astype(jnp.bfloat16), 'col')  49.5 us
  transfers between devices with their start and end apart: 13, of which 12 were waited for; matrix products, arithmetic and copies ran while one was open for 22% of the time, Pallas kernels for 0%

profile of v1, /device:TPU:1, one launch (start us, length us, event | category | flops | bytes accessed | tf_op | source)
XLA Modules:
  0.0 947.6 jit_solution(14010568968681377162)
XLA Ops:
  7.2 4.5 sort.45
  12.3 3.6 gather_fusion.1
  16.6 9.6 %all-to-all-start.1 = ((s32[32,16,1]{1,2,0:T(1,128)}), s32[32,16,1]{1,2,0:T(1,128)S(1)}, u32[]{:S(2)}, u32[]{:S(2)}) async-start(s32[32,16,1]{1,2,0:T(1,128)} %bitcast.2), calls=%async_computation.1 | async-start | bytes 32768 | tf_op jit(solution)/shard_map/all_to_all | solution.py:147
  26.2 2.6 gather_fusion
  28.9 4.2 all-to-all-done.1
  33.1 4.2 all-to-all-start
  38.6 3.8 sort.46
  42.4 6.5 all-to-all-done
  48.9 2.6 gather_fusion.2
  53.7 26.4 %all-gather.13.cloned.1.call-done = bf16[512,2048]{1,0:T(8,128)(2,1)} async-done(((bf16[512,512]{1,0:T(8,128)(2,1)}), bf16[512,2048]{1,0:T(8,128)(2,1)}) %all-gather.13.cloned.1.call-update) | async-done | bytes 2097168 | tf_op jit(solution)/shard_map/all_gather | solution.py:151
  80.0 2.1 fusion.54
  82.1 48.2 %all-gather.9.cloned.1.call-done = bf16[2048,1152]{1,0:T(8,128)(2,1)} async-done(((bf16[64,1152]{1,0:T(8,128)(2,1)}), bf16[2048,1152]{1,0:T(8,128)(2,1)}) %all-gather.9.cloned.1.call-update) | async-done | bytes 4718608 | tf_op jit(solution)/shard_map/all_gather | solution.py:99
  130.3 3.6 fusion.67
  135.6 1.9 convolution_bitcast_fusion.2
  138.0 2.0 fusion.72
  140.1 25.1 %while.32 = (s32[]{:T(128)}, bf16[8,512,64]{1,2,0:T(8,128)(2,1)S(1)}, f32[8,512]{1,0:T(8,128)}, bf16[8,512,64]{2,1,0:T(8,128)(2,1)}, bf16[1,512,64]{2,1,0:T(8,12...) while((s32[]{:T(128)}, bf16[8,512,64]{1,2,0:T(8,128)(2,1)S(1)}, ...), condition=%wide.region_8.9_spmd.clone.clone, body=%wide.region_5.8_spmd.clone.sunk.clone | while | flops 69991936 | bytes 3694689 | solution.py:178
  166.0 5.0 fusion.63
  172.0 2.0 gather_fusion.5
  174.0 16.6 %all_to_all.60 = bf16[32,16,512]{2,1,0:T(8,128)(2,1)S(1)} all-to-all(bf16[32,16,512]{2,1,0:T(8,128)(2,1)S(1)} %bitcast.186), channel_id=1, replica_groups=mesh['row'=32,'col'=4] {'row'}, dimensions={0} | all-to-all | bytes 1048576 | tf_op jit(solution)/shard_map/all_to_all | solution.py:146
  190.6 2.6 gather_fusion.6
  195.2 67.5 %all-reduce.3.cloned.1.call-done = f32[512,2048]{1,0:T(8,128)} async-done(((f32[512,2048]{1,0:T(8,128)}), f32[512,2048]{1,0:T(8,128)}) %all-reduce.3.cloned.1.call-update) | async-done | bytes 4194320 | tf_op jit(solution)/shard_map/psum | solution.py:194
  262.7 2.8 multiply_reduce_fusion.4
  265.6 2.0 copy-done.2
  269.3 26.3 %all-gather.15.cloned.1.call-done = bf16[512,2048]{1,0:T(8,128)(2,1)} async-done(((bf16[512,512]{1,0:T(8,128)(2,1)}), bf16[512,2048]{1,0:T(8,128)(2,1)}) %all-gather.15.cloned.1.call-update) | async-done | bytes 2097168 | tf_op jit(solution)/shard_map/all_gather | solution.py:152
  295.7 76.7 %all-gather.11.cloned.1.call-done = bf16[2048,4224]{1,0:T(8,128)(2,1)} async-done(((bf16[64,4224]{1,0:T(8,128)(2,1)}), bf16[2048,4224]{1,0:T(8,128)(2,1)}) %all-gather.11.cloned.1.call-update) | async-done | bytes 17301520 | tf_op jit(solution)/shard_map/all_gather | solution.py:99
  372.4 6.5 fusion.41
  378.9 2.3 copy-done.31
  381.3 5.0 fusion.47
  386.2 7.3 multiply_convert_fusion.4
  393.6 5.4 fusion.45
  398.9 5.0 fusion.55
  404.0 9.7 %all-gather.17.cloned.1.call-start = ((), (), s32[]{:S(2)}) async-start(), calls=%async_computation.14 | async-start | bytes 10485760 | tf_op jit(solution)/shard_map/all_gather | solution.py:254
  413.7 82.1 %all-reduce.5.cloned.1.call-done = f32[512,2048]{1,0:T(8,128)} async-done(((f32[512,2048]{1,0:T(8,128)}), f32[512,2048]{1,0:T(8,128)}) %all-reduce.5.cloned.1.call-update) | async-done | bytes 4194320 | tf_op jit(solution)/shard_map/psum | solution.py:217
  495.9 4.6 multiply_reduce_fusion.1
  501.8 2.7 multiply_add_fusion
  504.5 1.9 copy-done.7
  506.4 3.7 fusion.69
  511.6 50.9 %while.33 = (s32[]{:T(128)}, f32[8,512,64]{1,2,0:T(8,128)}, f32[8,512,64]{1,2,0:T(8,128)}, f32[8,512,64]{1,2,0:T(8,128)}, bf16[8,512,64]{2,1,0:T(8,128)(2,1)}, /...) while((s32[]{:T(128)}, f32[8,512,64]{1,2,0:T(8,128)}, ...), condition=%wide.region_17.18_spmd.clone.clone, body=%wide.region_15.17_spmd.clone.sunk.clone | while | flops 170982912 | bytes 9126013 | solution.py:224
  567.5 2.9 fusion.65
  572.2 3.2 add_convert_fusion
  575.5 7.9 fusion.58
  583.5 8.3 convolution_convert_fusion.2
  591.8 5.3 convolution_convert_fusion.1
  597.1 5.0 convolution_convert_fusion
  603.7 2.7 convolution_convert_fusion.4
  606.5 2.6 convolution_convert_fusion.3
  609.1 49.5 %all-gather.17.cloned.1.call-done = bf16[2048,2048]{1,0:T(8,128)(2,1)} async-done(((bf16[512,2048]{1,0:T(8,128)(2,1)}), bf16[2048,2048]{1,0:T(8,128)(2,1)}) %all-gather.17.cloned.1.call-update) | async-done | bytes 8388624 | tf_op jit(solution)/shard_map/all_gather | solution.py:254
  658.6 7.2 reduce_sum.109
  665.8 6.2 fusion.53
  672.0 93.2 %concatenate.53 = bf16[2048,5378]{0,1:T(8,128)(2,1)} concatenate(bf16[2048,512]{0,1:T(8,128)(2,1)} %convolution_convert_fusion.4, bf16[2048,64]{0,1:T(8,128)(2,1)S(1)} %convolution_convert_fusion.6, bf16[2048,64]{0,1:T(8,128)(2,1)S(1)} %convolution_convert_fusion.5, bf16[2048,512]{0,1:T(8,128)(2,1)} %convolution_convert_fusion.3, bf16[2048,1408]{0,1:T(8,128)(2,1)} %convolution_convert_fusion.2, ...), dimensions={1} | concatenate | bytes 44056576 | tf_op jit(solution)/shard_map/concatenate | solution.py:112
  765.2 28.4 %copy.67 = bf16[2048,5378]{1,0:T(8,128)(2,1)} copy(bf16[2048,5378]{0,1:T(8,128)(2,1)} %concatenate.53) | data formatting | bytes 44056576
  796.0 2.9 gather_fusion.3
  798.9 7.7 all-to-all-start.2
  806.6 2.5 fusion.73
  809.1 2.6 gather_fusion.7
  811.7 6.4 all-to-all-done.2
  818.1 4.0 all-to-all-start.4
  822.2 3.8 sort.47
  825.9 2.6 gather_fusion.4
  828.6 5.2 all-to-all-done.4
  833.8 2.6 gather_fusion.8
  836.4 90.7 %reduce-scatter.7.cloned.1.call-done = bf16[64,5378]{1,0:T(8,128)(2,1)} async-done(((bf16[2048,5378]{1,0:T(8,128)(2,1)}), bf16[64,5378]{1,0:T(8,128)(2,1)}) %reduce-scatter.7.cloned.1.call-update) | async-done | bytes 688400
  927.1 2.0 copy.68
  936.5 2.1 copy.64
  (249 shorter events, 111.2 us)
Async XLA Ops:
  7.2 19.0 %copy-start = (bf16[512,512]{1,0:T(8,128)(2,1)S(1)}, bf16[512,512]{1,0:T(8,128)(2,1)}, u32[]{:S(2)}) copy-start(bf16[512,512]{1,0:T(8,128)(2,1)} %param.17) | copy-start | bytes 1572868
  11.7 0.6 copy-start.28
  16.6 16.5 %all-to-all-start.1 = ((s32[32,16,1]{1,2,0:T(1,128)}), s32[32,16,1]{1,2,0:T(1,128)S(1)}, u32[]{:S(2)}, u32[]{:S(2)}) async-start(s32[32,16,1]{1,2,0:T(1,128)} %bitcast.2), calls=%async_computation.1 | async-start | bytes 32768 | tf_op jit(solution)/shard_map/all_to_all | solution.py:147
  28.9 22.8 %copy-start.19 = (bf16[64,512]{1,0:T(8,128)(2,1)S(1)}, bf16[64,512]{1,0:T(8,128)(2,1)}, u32[]{:S(2)}) copy-start(bf16[64,512]{1,0:T(8,128)(2,1)} %param.22) | copy-start | bytes 196612
  28.9 22.8 %copy-start.20 = (bf16[64,512]{1,0:T(8,128)(2,1)S(1)}, bf16[64,512]{1,0:T(8,128)(2,1)}, u32[]{:S(2)}) copy-start(bf16[64,512]{1,0:T(8,128)(2,1)} %param.25) | copy-start | bytes 196612
  28.9 22.8 %copy-start.21 = (bf16[64,64]{1,0:T(8,128)(2,1)S(1)}, bf16[64,64]{1,0:T(8,128)(2,1)}, u32[]{:S(2)}) copy-start(bf16[64,64]{1,0:T(8,128)(2,1)} %param.23) | copy-start | bytes 24580
  28.9 22.8 %copy-start.22 = (bf16[64,64]{1,0:T(8,128)(2,1)S(1)}, bf16[64,64]{1,0:T(8,128)(2,1)}, u32[]{:S(2)}) copy-start(bf16[64,64]{1,0:T(8,128)(2,1)} %param.24) | copy-start | bytes 24580
  28.9 23.7 %copy-start.25 = (s32[512]{0:T(512)S(1)}, s32[512]{0:T(512)}, u32[]{:S(2)}) copy-start(s32[512]{0:T(512)} %param.20) | copy-start | bytes 6148
  33.1 49.0 %copy-start.16 = (s32[32,16,1]{1,2,0:T(1,128)}, s32[32,16,1]{1,2,0:T(1,128)S(1)}, u32[]{:S(2)}) copy-start(s32[32,16,1]{1,2,0:T(1,128)S(1)} %all-to-all-done.1) | copy-start | bytes 6148
  33.1 15.9 %all-to-all-start = ((bf16[32,16,512]{2,1,0:T(8,128)(2,1)}), bf16[32,16,512]{2,1,0:T(8,128)(2,1)S(1)}, u32[]{:S(2)}, u32[]{:S(2)}) async-start(bf16[32,16,512]{2,1,0:T(8,128)(2,1)} %bitcast), calls=%async_computation | async-start | bytes 1048576 | tf_op jit(solution)/shard_map/all_to_all | solution.py:145
  37.3 42.7 %all-gather.13.cloned.1.call-start = ((), (), s32[]{:S(2)}) async-start(), calls=%async_computation.12 | async-start | bytes 2621440 | tf_op jit(solution)/shard_map/all_gather | solution.py:151
  48.9 81.4 %copy-start.23 = (f32[2048]{0:T(1024)S(1)}, f32[2048]{0:T(1024)}, u32[]{:S(2)}) copy-start(f32[2048]{0:T(1024)} %param.21) | copy-start | bytes 24580
  51.6 78.8 %all-gather.9.cloned.1.call-start = ((), (), s32[]{:S(2)}) async-start(), calls=%async_computation.7 | async-start | bytes 4866048 | tf_op jit(solution)/shard_map/all_gather | solution.py:99
  52.5 210.3 %all-reduce.3.cloned.1.call-start = ((), (), s32[]{:S(2)}) async-start(), calls=%async_computation.8 | async-start | bytes 8388608 | tf_op jit(solution)/shard_map/psum | solution.py:194
  53.1 84.4 %copy-start.30 = (f32[32]{0:T(128)}, f32[32]{0:T(128)S(1)}, u32[]{:S(2)}) copy-start(f32[32]{0:T(128)S(1)} %negate_power_fusion) | copy-start | bytes 388
  134.0 1.7 copy-start.5
  135.6 4.5 copy-start.26
  165.2 0.8 copy-start.9
  171.0 1.0 copy-start.4
  171.0 124.6 %all-gather.15.cloned.1.call-start = ((), (), s32[]{:S(2)}) async-start(), calls=%async_computation.13 | async-start | bytes 2621440 | tf_op jit(solution)/shard_map/all_gather | solution.py:152
  190.6 2.7 copy-start.14
  190.6 2.7 copy-start.15
  193.3 179.1 %all-gather.11.cloned.1.call-start = ((), (), s32[]{:S(2)}) async-start(), calls=%async_computation.9 | async-start | bytes 17842176 | tf_op jit(solution)/shard_map/all_gather | solution.py:99
  195.1 72.5 %copy-start.18 = (f32[2048]{0:T(1024)S(1)}, f32[2048]{0:T(1024)}, u32[]{:S(2)}) copy-start(f32[2048]{0:T(1024)} %param.26) | copy-start | bytes 24580
  195.2 300.7 %all-reduce.5.cloned.1.call-start = ((), (), s32[]{:S(2)}) async-start(), calls=%async_computation.11 | async-start | bytes 8388608 | tf_op jit(solution)/shard_map/psum | solution.py:217
  265.6 2.1 copy-start.2
  372.4 6.6 copy-start.11
  372.4 8.9 copy-start.31
  393.6 5.4 copy-start.32
  404.0 254.6 %all-gather.17.cloned.1.call-start = ((), (), s32[]{:S(2)}) async-start(), calls=%async_computation.14 | async-start | bytes 10485760 | tf_op jit(solution)/shard_map/all_gather | solution.py:254
  495.9 4.6 copy-start.3
  495.9 5.9 copy-start.6
  504.4 1.9 copy-start.7
  506.4 5.2 copy-start.27
  575.5 219.0 %reduce-scatter.5.cloned.1.call-start = ((), (), s32[]{:S(2)}) async-start(), calls=%async_computation.10 | async-start | bytes 2621440 | tf_op jit(solution)/shard_map/reduce_scatter | solution.py:204
  583.4 343.7 %reduce-scatter.7.cloned.1.call-start = ((), (), s32[]{:S(2)}) async-start(), calls=%async_computation.15 | async-start | bytes 23248896
  583.5 8.3 copy-start.12
  583.5 8.3 copy-start.34
  591.8 5.3 copy-start.13
  591.8 5.3 copy-start.33
  597.1 5.0 copy-start.24
  603.7 2.8 copy-start.8
  603.7 2.7 copy-start.10
  793.6 0.7 copy-start.17
  798.9 19.3 %all-to-all-start.2 = ((bf16[32,16,512]{2,1,0:T(8,128)(2,1)}), bf16[32,16,512]{2,1,0:T(8,128)(2,1)S(1)}, u32[]{:S(2)}, u32[]{:S(2)}) async-start(bf16[32,16,512]{2,1,0:T(8,128)(2,1)} %bitcast.14), calls=%async_computation.3 | async-start | bytes 1048576 | tf_op jit(solution)/shard_map/all_to_all | solution.py:283
  806.6 15.6 %copy-start.29 = (s32[512]{0:T(512)S(1)}, s32[512]{0:T(512)}, u32[]{:S(2)}) copy-start(s32[512]{0:T(512)} %copy-done.28) | copy-start | bytes 6148
  818.1 15.7 %all-to-all-start.4 = ((bf16[32,16,512]{2,1,0:T(8,128)(2,1)}), bf16[32,16,512]{2,1,0:T(8,128)(2,1)S(1)}, u32[]{:S(2)}, u32[]{:S(2)}) async-start(bf16[32,16,512]{2,1,0:T(8,128)(2,1)} %bitcast.25), calls=%async_computation.5 | async-start | bytes 1048576 | tf_op jit(solution)/shard_map/all_to_all | solution.py:284
  930.1 10.4 %copy-start.1 = (bf16[512,512]{1,0:T(8,128)(2,1)S(1)}, bf16[512,512]{1,0:T(8,128)(2,1)}, u32[]{:S(2)}) copy-start(bf16[512,512]{1,0:T(8,128)(2,1)} %param.17) | copy-start | bytes 1572868
Sparse Core Ops, SparseCore 0:
  51.7 28.2 all-gather.12
  82.8 47.4 all-gather.8
  171.1 91.5 all-reduce.2
  264.9 30.6 all-gather.14
  298.0 74.3 all-gather.10
  404.1 91.7 all-reduce.4
  575.6 82.9 all-gather.16
  661.0 30.6 reduce-scatter.4
  793.8 133.3 reduce-scatter.6
